TPU v7x, 256 devices: a whole 4x4x8 slice. The times are simulated.
256 devices in a mesh: island: 16 (over y_hi, z), inner: 16 (over y_lo, x, core).
Axes of the slice: x: 4, y: 4 (y_hi: 2, y_lo: 2; y = y_hi * 2 + y_lo), z: 8, core: 2. Of those that a mesh axis runs over, the one named last changes fastest.
Arguments:
- island_delta: float32 [16, 2, 8192, 512], P('island', None, 'inner'), may hold values from -200 to 200, as said below
- params: float32 [2, 8192, 512], P(None, 'inner'), may hold values from -6 to 6
- momentum: float32 [2, 8192, 512], P(None, 'inner'), may hold values from -6 to 6
Outputs:
- new_params: float32 [2, 8192, 512], P(None, 'inner')
- new_momentum: float32 [2, 8192, 512], P(None, 'inner')
Inputs may be any that keep to these rules, and one draw needn't show every extreme that they name: `island_delta`: entries are finite and of mixed sign.
All inputs are finite; a program needn't handle non-finite values.
Results may differ from a plain program's by a relative error of at most 0.0003.
Values sent between devices are 32-bit elements; how exact they have to be, the bound alone decides.
A program may use at most 64 MiB of HBM per device.

v0:
```python
import jax
import jax.numpy as jnp
from jax import lax
from jax.sharding import PartitionSpec as P

D = 8192
HEAD = 128
KVH = 4


def outer_update(average, params, momentum, mean_square):
    factor = jnp.minimum(jnp.float32(1.0), 0.5 / jnp.sqrt(mean_square + 1e-06))
    clipped = factor * average
    new_momentum = 0.9 * momentum + clipped
    new_params = params - 0.7 * (clipped + 0.9 * new_momentum)
    return (new_params, new_momentum)


def body(island_delta, params, momentum):
    replicas = lax.axis_size("island")
    count = 2 * D * KVH * HEAD
    own_delta = island_delta[0]
    average = lax.psum(own_delta, "island") / replicas
    total_sq = lax.psum(jnp.sum(average * average), "inner")
    return outer_update(average, params, momentum, total_sq / count)


def solution(mesh):
    in_specs = (P("island", None, "inner", None), P(None, "inner", None), P(None, "inner", None))
    out_specs = (P(None, "inner", None), P(None, "inner", None))
    return jax.shard_map(body, mesh=mesh, in_specs=in_specs, out_specs=out_specs, check_vma=False)
```

profile of v0, /device:TPU:1, one launch (start us, length us, event | category | flops | bytes accessed | tf_op | source)
XLA Modules:
  0.0 220.7 jit_solution(3867526521445673255)
XLA Ops:
  7.2 0.0 all-reduce.2.cloned.1.call-start
  7.2 0.7 all-reduce.2.cloned.1.call-update
  7.9 158.7 %all-reduce.2.cloned.1.call-done = f32[2,512,512]{2,1,0:T(8,128)} async-done(((f32[2,512,512]{2,1,0:T(8,128)}), f32[2,512,512]{2,1,0:T(8,128)}) %all-reduce.2.cloned.1.call-update) | async-done | bytes 2097168 | tf_op jit(solution)/shard_map/psum | solution.py:23
  166.6 0.0 copy-start
  166.6 2.9 %multiply_reduce_fusion = f32[]{:T(128)} fusion(f32[2,512,512]{2,1,0:T(8,128)} %all-reduce.2.cloned.1.call-done), kind=kLoop, calls=%fused_computation.2 | loop fusion | flops 1572863 | bytes 2097156 | tf_op jit(solution)/shard_map/reduce_sum | solution.py:24
  169.5 38.6 %psum.15 = f32[]{:T(128)} all-reduce(f32[]{:T(128)} %multiply_reduce_fusion), channel_id=1, replica_groups=mesh['island'=16,'inner'=16] {'inner'}, use_global_device_ids=true, to_apply=%region_2.0 | all-reduce | flops 1 | bytes 8 | tf_op jit(solution)/shard_map/psum | solution.py:24
  208.9 0.0 copy-done
  208.9 5.0 %multiply_subtract_fusion = (f32[2,512,512]{2,1,0:T(8,128)}, f32[2,512,512]{2,1,0:T(8,128)}) fusion(f32[2,512,512]{2,1,0:T(8,128)} %param.4, f32[2,512,512]{2,1,0:T(8,128)S(1)} %copy-done, f32[]{:T(128)S(6)} %mul.24, f32[2,512,512]{2,1,0:T(8,128)} %param.5), kind=kLoop, calls=%fused_computation | loop fusion | flops 3670016 | bytes 10485764 | tf_op jit(solution)/shard_map/sub | solution.py:15
Async XLA Ops:
  7.2 159.5 %all-reduce.2.cloned.1.call-start = ((), (), s32[]{:S(2)}) async-start(), calls=%async_computation | async-start | bytes 4194304 | tf_op jit(solution)/shard_map/psum | solution.py:23
  166.6 42.2 %copy-start = (f32[2,512,512]{2,1,0:T(8,128)S(1)}, f32[2,512,512]{2,1,0:T(8,128)}, u32[]{:S(2)}) copy-start(f32[2,512,512]{2,1,0:T(8,128)} %all-reduce.2.cloned.1.call-done) | copy-start | bytes 6291460
Sparse Core Ops, SparseCore 0:
  10.6 155.9 all-reduce.1
where the time goes:
time: 221 us
  waiting for transfers between devices  159 us (72%)
  blocking collectives  38.6 us (17%)
  between operations  14.7 us (7%)
  other arithmetic  7.91 us (4%)
    psum x1, waiting for transfers between devices, body(): average = lax.psum(own_delta, 'island') / replicas  159 us
    psum x1, blocking collectives, body(): total_sq = lax.psum(jnp.sum(average * average), 'inner')  38.6 us
    sub x1, other arithmetic, outer_update(): new_params = params - 0.7 * (clipped + 0.9 * new_momentum)  5.02 us
  transfers between devices with their start and end apart: 1, of which 1 were waited for; matrix products, arithmetic and copies ran while one was open for 0% of the time, Pallas kernels for 0%

commit v1 on v0

--- a/solution.py
+++ b/solution.py
@@ -20,7 +20,7 @@
     replicas = lax.axis_size("island")
     count = 2 * D * KVH * HEAD
     own_delta = island_delta[0]
-    average = lax.psum(own_delta, "island") / replicas
+    average = jnp.sum(lax.all_gather(own_delta, "island"), axis=0) / replicas
     total_sq = lax.psum(jnp.sum(average * average), "inner")
     return outer_update(average, params, momentum, total_sq / count)
 

time: 221 us -> 482 us (2.18)
  waiting for transfers between devices: 159 us -> 419 us
  other arithmetic: 7.91 us -> 18.9 us
  blocking collectives: 38.6 us -> 28.5 us
    all_gather x0 -> x1, waiting for transfers between devices: none -> 418 us  [body(): average = jnp.sum(lax.all_gather(own_delta, 'island'), axis=0) / replicas]
    psum x1 -> x0, waiting for transfers between devices: 159 us -> none  [body(): average = lax.psum(own_delta, 'island') / replicas]
    reduce_sum x0 -> x1, other arithmetic: none -> 12.7 us  [body(): average = jnp.sum(lax.all_gather(own_delta, 'island'), axis=0) / replicas]
    psum x1, blocking collectives: 38.6 us -> 28.5 us  [body(): total_sq = lax.psum(jnp.sum(average * average), 'inner')]
where the time goes in v1:
time: 482 us; the launch traced here: 481 us
  waiting for transfers between devices  419 us (87%)
  blocking collectives  28.5 us (6%)
  other arithmetic  18.9 us (4%)
  between operations  14.7 us (3%)
    all_gather x1, waiting for transfers between devices, body(): average = jnp.sum(lax.all_gather(own_delta, 'island'), axis=0) / replicas  418 us
    psum x1, blocking collectives, body(): total_sq = lax.psum(jnp.sum(average * average), 'inner')  28.5 us
    reduce_sum x1, other arithmetic, body(): average = jnp.sum(lax.all_gather(own_delta, 'island'), axis=0) / replicas  12.7 us
  transfers between devices with their start and end apart: 1, of which 1 were waited for; matrix products, arithmetic and copies ran while one was open for 0% of the time, Pallas kernels for 0%

profile of v1, /device:TPU:1, one launch (start us, length us, event | category | flops | bytes accessed | tf_op | source)
XLA Modules:
  0.0 481.2 jit_solution(12447380771022578183)
XLA Ops:
  7.2 0.0 all-gather.2.cloned.1.call-start
  7.2 0.7 all-gather.2.cloned.1.call-update
  7.9 418.3 %all-gather.2.cloned.1.call-done = f32[16,2,512,512]{3,2,1,0:T(8,128)} async-done(((f32[1,2,512,512]{3,2,1,0:T(8,128)}), f32[16,2,512,512]{3,2,1,0:T(8,128)}) %all-gather.2.cloned.1.call-update) | async-done | bytes 33554448 | tf_op jit(solution)/shard_map/all_gather | solution.py:23
  426.2 12.7 %reduce_sum.18 = f32[2,512,512]{2,1,0:T(8,128)S(1)} reduce(f32[16,2,512,512]{3,2,1,0:T(8,128)} %all-gather.2.cloned.1.call-done, f32[]{:T(128)} %constant.2.clone.1), dimensions={0}, to_apply=%region_0.0 | reduce | flops 7864320 | bytes 35651588 | tf_op jit(solution)/shard_map/reduce_sum | solution.py:23
  439.0 1.1 multiply_reduce_fusion
  440.1 28.5 %psum.7 = f32[]{:T(128)} all-reduce(f32[]{:T(128)} %multiply_reduce_fusion), channel_id=1, replica_groups=mesh['island'=16,'inner'=16] {'inner'}, use_global_device_ids=true, to_apply=%region_2.0 | all-reduce | flops 1 | bytes 8 | tf_op jit(solution)/shard_map/psum | solution.py:24
  469.3 5.0 %multiply_subtract_fusion = (f32[2,512,512]{2,1,0:T(8,128)}, f32[2,512,512]{2,1,0:T(8,128)}) fusion(f32[2,512,512]{2,1,0:T(8,128)} %param.4, f32[2,512,512]{2,1,0:T(8,128)S(1)} %reduce_sum.18, f32[]{:T(128)S(6)} %mul.24, f32[2,512,512]{2,1,0:T(8,128)} %param.5), kind=kLoop, calls=%fused_computation | loop fusion | flops 3670016 | bytes 10485764 | tf_op jit(solution)/shard_map/sub | solution.py:15
Async XLA Ops:
  7.2 419.1 %all-gather.2.cloned.1.call-start = ((), (), s32[]{:S(2)}) async-start(), calls=%async_computation | async-start | bytes 35651584 | tf_op jit(solution)/shard_map/all_gather | solution.py:23
Sparse Core Ops, SparseCore 0:
  10.6 415.6 all-gather.1
